TPU v7x, 32 devices: a whole 2x2x4 slice. The times are simulated.
32 devices in a mesh: illum: 2 (over y), gx: 4 (over x, core), gy: 4 (over z).
Axes of the slice: x: 2, y: 2, z: 4, core: 2. Of those that a mesh axis runs over, the one named last changes fastest.
Arguments:
- density: float32 [128, 64, 128], P('gx', 'gy'), may hold values from 0 to 1
- moment_one: float32 [128, 64, 128], P('gx', 'gy'), may hold values from -0.6 to 0.6
- moment_two: float32 [128, 64, 128], P('gx', 'gy'), may hold values from 0.0002 to 0.0006
- forward_field: bfloat16 [2, 2, 3, 128, 64, 128], P('illum', None, None, 'gx', 'gy'), may hold values from -6 to 6
- adjoint_field: bfloat16 [2, 2, 3, 128, 64, 128], P('illum', None, None, 'gx', 'gy'), may hold values from -6 to 6
- objective_weight: float32 [2], P('illum'), may hold values from 0.02 to 0.2
Outputs:
- new_density: float32 [128, 64, 128], P('gx', 'gy')
- new_moment_one: float32 [128, 64, 128], P('gx', 'gy')
- new_moment_two: float32 [128, 64, 128], P('gx', 'gy')
- physical: float32 [128, 64, 128], P('gx', 'gy')
All inputs are finite; a program needn't handle non-finite values.
Results may differ from a plain program's by a relative error of at most 0.0003.
Values sent between devices are 32-bit elements; how exact they have to be, the bound alone decides.
A program may use at most 64 MiB of HBM per device.

v0:
```python
import functools
import math

import jax
import jax.numpy as jnp
from jax import lax
from jax.experimental import pallas as pl
from jax.experimental.pallas import tpu as pltpu
from jax.sharding import PartitionSpec as P

RADIUS = 8
SHARPNESS = 8.0
THRESHOLD = 0.5
TANH_EDGE = math.tanh(SHARPNESS * THRESHOLD)
SCALE = math.tanh(SHARPNESS * THRESHOLD) + math.tanh(SHARPNESS * (1.0 - THRESHOLD))
NORM = 1.0 / float((RADIUS + 1) ** 6)
FIRST_FIX = 1.0 / (1.0 - 0.9**5)
SECOND_FIX = 1.0 / (1.0 - 0.999**5)
MESH = pl.DeviceIdType.MESH
ROUNDS = 3


def split(value):
    high = value.astype(jnp.bfloat16)
    low = (value - high.astype(jnp.float32)).astype(jnp.bfloat16)
    return high, low


def box(value):
    n = value.shape[0]
    two = value[: n - 1] + value[1:]
    four = two[: n - 3] + two[2:]
    eight = four[: n - 7] + four[4:]
    return eight[: n - 8] + value[8:]


def depth_matrix(length):
    row = lax.broadcasted_iota(jnp.int32, (2 * length, length), 0)
    col = lax.broadcasted_iota(jnp.int32, (2 * length, length), 1)
    row = jnp.where(row >= length, row - length, row)
    taps = jnp.maximum(RADIUS + 1 - jnp.abs(row - col), 0)
    return taps.astype(jnp.float32).astype(jnp.bfloat16)


def kernel(
    sizes,
    den,
    m1,
    m2,
    fwd,
    adj,
    weight,
    new_den,
    new_m1,
    new_m2,
    physical,
    ybuf,
    xbuf,
    sens,
    fbuf,
    abuf,
    m1buf,
    m2buf,
    filt,
    local_sem,
    y_send,
    y_recv,
    x_send,
    x_recv,
    s_send,
    s_recv,
):
    n_illum, n_gx, n_gy = sizes
    tile_x, tile_y, depth = den.shape
    sources, _, comps = fwd.shape[:3]
    me = lax.axis_index("illum")
    gx = lax.axis_index("gx")
    gy = lax.axis_index("gy")
    side = (gx < n_gx // 2).astype(jnp.int32)
    reach = tile_x - RADIUS
    pieces = [
        (side * reach, RADIUS),
        ((1 - side) * reach, RADIUS),
        (RADIUS, tile_x - 2 * RADIUS),
    ]
    own = pl.ds(RADIUS, tile_y)

    loads = {}

    def load(name, src, dst):
        copy = pltpu.make_async_copy(src, dst, local_sem.at[len(loads)])
        copy.start()
        loads[name] = copy

    for i, (p, n) in enumerate(pieces):
        part = pl.ds(p, n)
        load(("f", i), fwd.at[:, :, :, part], fbuf.at[:, :, :, part])
        load(("a", i), adj.at[:, :, :, part], abuf.at[:, :, :, part])
    load("d", den, ybuf.at[0, :, own])
    load("m1", m1, m1buf)
    load("m2", m2, m2buf)

    near, far = gx + 2 * side - 1, gx - 2 * side + 1
    x_sides = [
        (jnp.logical_and(at >= 0, at < n_gx), {"gx": jnp.clip(at, 0, n_gx - 1)})
        for at in (near, far)
    ]
    y_prev = (gy > 0, {"gy": jnp.maximum(gy - 1, 0)})
    y_next = (gy < n_gy - 1, {"gy": jnp.minimum(gy + 1, n_gy - 1)})
    others = [{"illum": lax.rem(me + k, n_illum)} for k in range(1, n_illum)]

    barrier = pltpu.get_barrier_semaphore()
    for there, device in (y_prev, y_next, *x_sides):

        @pl.when(there)
        def _(device=device):
            pl.semaphore_signal(barrier, inc=1, device_id=device, device_id_type=MESH)

    for device in others:
        pl.semaphore_signal(barrier, inc=1, device_id=device, device_id_type=MESH)
    for there, land in ((y_prev[0], 0), (y_next[0], RADIUS + tile_y)):

        @pl.when(jnp.logical_not(there))
        def _(land=land):
            for r in range(ROUNDS):
                ybuf[r, :, pl.ds(land, RADIUS)] = jnp.zeros(
                    (tile_x, RADIUS, depth), jnp.float32
                )

    for there, land in ((gx > 0, 0), (gx < n_gx - 1, RADIUS + tile_x)):

        @pl.when(jnp.logical_not(there))
        def _(land=land):
            for r in range(ROUNDS):
                xbuf[r, pl.ds(land, RADIUS)] = jnp.zeros(
                    (RADIUS, tile_y, depth), jnp.float32
                )

    group = RADIUS
    z_taps = depth_matrix(depth)

    peers = jnp.int32(len(others))
    for there, _ in (y_prev, y_next, *x_sides):
        peers = peers + there.astype(jnp.int32)
    pl.semaphore_wait(barrier, peers)

    def y_copy(r, d, i, source=None):
        p, n = pieces[i]
        part = pl.ds(p, n)
        if d == 0:
            rows, land, device = RADIUS, RADIUS + tile_y, y_prev[1]
        else:
            rows, land, device = tile_y, 0, y_next[1]
        if source is None:
            src = ybuf.at[r, part, pl.ds(rows, RADIUS)]
        else:
            src = source.at[part, pl.ds(rows - RADIUS, RADIUS)]
        return pltpu.make_async_remote_copy(
            src_ref=src,
            dst_ref=ybuf.at[r, part, pl.ds(land, RADIUS)],
            send_sem=y_send.at[r, d, i],
            recv_sem=y_recv.at[r, d, i],
            device_id=device,
            device_id_type=MESH,
        )

    def x_copy(r, i, back=False):
        start = pieces[i][0]
        high = side if i == 0 else 1 - side
        if back:
            land = high * (tile_x + RADIUS)
        else:
            land = (1 - high) * (tile_x + RADIUS)
        sent, got = (1 - high, high)
        return pltpu.make_async_remote_copy(
            src_ref=xbuf.at[r, pl.ds(RADIUS + start, RADIUS)],
            dst_ref=xbuf.at[r, pl.ds(land, RADIUS)],
            send_sem=x_send.at[r, i],
            recv_sem=x_recv.at[r, got if back else sent],
            device_id=x_sides[i][1],
            device_id_type=MESH,
        )

    def s_copy(k, i):
        part = pl.ds(*pieces[i])
        return pltpu.make_async_remote_copy(
            src_ref=sens.at[me, part],
            dst_ref=sens.at[me, part],
            send_sem=s_send.at[k, i],
            recv_sem=s_recv.at[k, i],
            device_id=others[k],
            device_id_type=MESH,
        )

    def y_start(r, i, source=None):
        for d, (there, _) in enumerate((y_prev, y_next)):

            @pl.when(there)
            def _(d=d):
                y_copy(r, d, i, source).start()

    def y_arrive(r, i):
        for d, (there, _) in enumerate((y_next, y_prev)):

            @pl.when(there)
            def _(d=d):
                y_copy(r, d, i).wait_recv()

    for i in range(len(pieces)):
        y_start(0, i, den)

    for i, (p, n) in enumerate(pieces):
        loads["f", i].wait()
        loads["a", i].wait()
        for q in [p + j for j in range(n)]:
            total = None
            for s in range(sources):
                real, imag = None, None
                for c in range(comps):
                    a = fbuf[s, 0, c, q].astype(jnp.float32) * abuf[s, 0, c, q].astype(
                        jnp.float32
                    )
                    b = fbuf[s, 1, c, q].astype(jnp.float32) * abuf[s, 1, c, q].astype(
                        jnp.float32
                    )
                    real = (a - b) if real is None else real + (a - b)
                term = weight[s] * real
                total = term if total is None else total + term
            sens[me, q] = total
        for k in range(len(others)):
            s_copy(k, i).start()

    def y_filter(r, i):
        p, n = pieces[i]
        for g in [p + j for j in range(0, n, group)]:
            total = None
            for k in range(RADIUS + 1):
                row = ybuf[r, pl.ds(g, group), pl.ds(k, tile_y)]
                if k < RADIUS:
                    row = row + ybuf[
                        r, pl.ds(g, group), pl.ds(2 * RADIUS - k, tile_y)
                    ]
                row = row * float(k + 1)
                total = row if total is None else total + row
            xbuf[r, pl.ds(RADIUS + g, group)] = total

    def xz_filter(r, i):
        p, n = pieces[i]
        halves = []
        for h in range(0, tile_y, 8):
            value = xbuf[r, pl.ds(p, n + 2 * RADIUS), pl.ds(h, 8)]
            halves.append(box(box(value)))
        value = jnp.concatenate(halves, axis=1).reshape(n * tile_y, depth)
        both = jnp.concatenate(split(value), axis=1)
        out = jnp.dot(both, z_taps, preferred_element_type=jnp.float32)
        return (out * NORM).reshape(n, tile_y, depth)

    def through_x(r):
        for i in (0, 1):
            y_arrive(r, i)
            y_filter(r, i)
            there = x_sides[i][0]

            @pl.when(there)
            def _(i=i):
                x_copy(r, i).start()

        y_arrive(r, 2)
        y_filter(r, 2)

    def x_arrive(r, i):
        there = x_sides[i][0]

        @pl.when(there)
        def _():
            x_copy(r, i, back=True).wait_recv()

    def chain(i, filtered):
        p, n = pieces[i]
        part = pl.ds(p, n)
        for k in range(len(others)):
            source = lax.rem(me + n_illum - 1 - k, n_illum)
            pltpu.make_async_remote_copy(
                src_ref=sens.at[me, part],
                dst_ref=sens.at[source, part],
                send_sem=s_send.at[k, i],
                recv_sem=s_recv.at[k, i],
                device_id=others[k],
                device_id_type=MESH,
            ).wait_recv()
        total = sens[0, part]
        for e in range(1, n_illum):
            total = total + sens[e, part]
        inner = jnp.tanh(SHARPNESS * (filtered - THRESHOLD))
        ybuf[1, part, own] = total * (
            SHARPNESS * (1.0 - inner * inner) * (1.0 / SCALE)
        )
        y_start(1, i)

    def update(i, gradient):
        part = pl.ds(*pieces[i])
        one = 0.9 * m1buf[part] + 0.1 * gradient
        two = 0.999 * m2buf[part] + 0.001 * gradient * gradient
        new_m1[part] = one
        new_m2[part] = two
        step = one * FIRST_FIX / (jnp.sqrt(two * SECOND_FIX) + 1e-08)
        value = jnp.clip(ybuf[0, part, own] - 0.05 * step, 0.0, 1.0)
        ybuf[2, part, own] = value
        y_start(2, i)
        new_den[part] = value

    def finish(i, value):
        part = pl.ds(*pieces[i])
        physical[part] = (TANH_EDGE + jnp.tanh(SHARPNESS * (value - THRESHOLD))) * (
            1.0 / SCALE
        )

    loads["d"].wait()
    through_x(0)
    filt[...] = xz_filter(0, 2)
    for i in (0, 1):
        x_arrive(0, i)
        chain(i, xz_filter(0, i))
    chain(2, filt[...])

    loads["m1"].wait()
    loads["m2"].wait()
    through_x(1)
    filt[...] = xz_filter(1, 2)
    for i in (0, 1):
        x_arrive(1, i)
        update(i, xz_filter(1, i))
    update(2, filt[...])
    through_x(2)
    finish(2, xz_filter(2, 2))
    for i in (1, 0):
        x_arrive(2, i)
        finish(i, xz_filter(2, i))

    for i in range(len(pieces)):
        for k in range(len(others)):
            s_copy(k, i).wait_send()
    for d in (0, 1):

        @pl.when((y_prev, y_next)[d][0])
        def _(d=d):
            for r in range(ROUNDS):
                for i in range(len(pieces)):
                    y_copy(r, d, i, den if r == 0 else None).wait_send()

        @pl.when(x_sides[d][0])
        def _(d=d):
            for r in range(ROUNDS):
                x_copy(r, d).wait_send()


def export(a, b, c, d, a_out, b_out, c_out, d_out, sem):
    copies = [
        pltpu.make_async_copy(src, dst, sem.at[i])
        for i, (src, dst) in enumerate(
            ((a, a_out), (b, b_out), (c, c_out), (d, d_out))
        )
    ]
    for copy in copies:
        copy.start()
    for copy in copies:
        copy.wait()


def shards(sizes, density, moment_one, moment_two, forward_field, adjoint_field, objective_weight):
    tile_x, tile_y, depth = density.shape
    n_illum = sizes[0]
    tile = jax.ShapeDtypeStruct(density.shape, jnp.float32)
    f32 = jnp.float32
    far = max(n_illum - 1, 1)
    arguments = [
        pltpu.with_memory_space_constraint(x, pltpu.HBM)
        for x in (density, moment_one, moment_two, forward_field, adjoint_field)
    ]
    results = pl.pallas_call(
        functools.partial(kernel, sizes),
        out_shape=(pltpu.VMEM(density.shape, f32),) * 4,
        in_specs=[pl.BlockSpec(memory_space=pltpu.HBM)] * 5
        + [pl.BlockSpec(memory_space=pltpu.SMEM)],
        out_specs=(pl.BlockSpec(memory_space=pltpu.VMEM),) * 4,
        scratch_shapes=[
            pltpu.VMEM((ROUNDS, tile_x, tile_y + 2 * RADIUS, depth), f32),
            pltpu.VMEM((ROUNDS, tile_x + 2 * RADIUS, tile_y, depth), f32),
            pltpu.VMEM((n_illum, tile_x, tile_y, depth), f32),
            pltpu.VMEM(forward_field.shape, forward_field.dtype),
            pltpu.VMEM(adjoint_field.shape, adjoint_field.dtype),
            pltpu.VMEM(density.shape, f32),
            pltpu.VMEM(density.shape, f32),
            pltpu.VMEM((tile_x - 2 * RADIUS, tile_y, depth), f32),
            pltpu.SemaphoreType.DMA((9,)),
            pltpu.SemaphoreType.DMA((ROUNDS, 2, 3)),
            pltpu.SemaphoreType.DMA((ROUNDS, 2, 3)),
            pltpu.SemaphoreType.DMA((ROUNDS, 2)),
            pltpu.SemaphoreType.DMA((ROUNDS, 2)),
            pltpu.SemaphoreType.DMA((far, 3)),
            pltpu.SemaphoreType.DMA((far, 3)),
        ],
        compiler_params=pltpu.CompilerParams(
            collective_id=0, has_side_effects=True, vmem_limit_bytes=48 << 20
        ),
        name="design_update",
    )(*arguments, objective_weight)
    return pl.pallas_call(
        export,
        out_shape=(tile,) * 4,
        in_specs=[pl.BlockSpec(memory_space=pltpu.VMEM)] * 4,
        out_specs=(pl.BlockSpec(memory_space=pl.ANY),) * 4,
        scratch_shapes=[pltpu.SemaphoreType.DMA((4,))],
        compiler_params=pltpu.CompilerParams(vmem_limit_bytes=4 << 20),
        name="export_results",
    )(*results)


def solution(mesh):
    field = P("illum", None, None, "gx", "gy", None)
    tile = P("gx", "gy", None)
    sizes = (mesh.shape["illum"], mesh.shape["gx"], mesh.shape["gy"])
    return jax.shard_map(
        functools.partial(shards, sizes),
        mesh=mesh,
        in_specs=(tile, tile, tile, field, field, P("illum")),
        out_specs=(tile,) * 4,
        check_vma=False,
    )
```

profile of v0, /device:TPU:1, one launch (start us, length us, event | category | flops | bytes accessed | tf_op | source)
XLA Modules:
  0.0 26.0 jit_solution(11244860966653901488)
XLA Ops:
  1.3 23.7 %design_update.1 = (f32[32,16,128]{2,1,0:T(8,128)S(1)}, f32[32,16,128]{2,1,0:T(8,128)S(1)}, f32[32,16,128]{2,1,0:T(8,128)S(1)}, f32[32,16,128]{2,1,0:T(8,128)S(1)}) custom-call(f32[32,16,128]{2,1,0:T(8,128)} %den.1, f32[32,16,128]{2,1,0:T(8,128)} %m1.1, f32[32,16,128]{2,1,0:T(8,128)} %m2.1, bf16[1,2,3,32,16,128]{5,4,3,2,1,0:T(8,128)(2,1)} %fwd.1, ...), custom_call_target="tpu_custom_call" | custom-call | tf_op jit(solution)/shard_map/design_update/pallas_call | solution.py:380
  25.0 1.0 %export_results.1 = (f32[32,16,128]{2,1,0:T(8,128)}, f32[32,16,128]{2,1,0:T(8,128)}, f32[32,16,128]{2,1,0:T(8,128)}, f32[32,16,128]{2,1,0:T(8,128)}) custom-call(f32[32,16,128]{2,1,0:T(8,128)S(1)} %get-tuple-element.8.a, f32[32,16,128]{2,1,0:T(8,128)S(1)} %get-tuple-element.9.b, f32[32,16,128]{2,1,0:T(8,128)S(1)} %get-tuple-element.10.c, ...), custom_call_target="tpu_custom_call" | custom-call | tf_op jit(solution)/shard_map/export_results/pallas_call | solution.py:408
where the time goes:
time: 26.2 us; the launch traced here: 26 us
  Pallas kernels  24.7 us (94%)
  between operations  1.29 us (5%)
    pallas_call x1, Pallas kernels, shards(): pl.pallas_call(functools.partial(kernel, sizes), out_shape=(pltpu.VMEM(de...  23.7 us
    pallas_call x1, Pallas kernels, shards(): pl.pallas_call(export, out_shape=(tile,) * 4, in_specs=[pl.BlockSpec(memo...  1 us

commit v1 on v0

v1 whole, which is shorter than its diff:
```python
import functools
import math

import jax
import jax.numpy as jnp
from jax import lax
from jax.experimental import pallas as pl
from jax.experimental.pallas import tpu as pltpu
from jax.sharding import PartitionSpec as P

RADIUS = 8
SHARPNESS = 8.0
THRESHOLD = 0.5
TANH_EDGE = math.tanh(SHARPNESS * THRESHOLD)
SCALE = math.tanh(SHARPNESS * THRESHOLD) + math.tanh(SHARPNESS * (1.0 - THRESHOLD))
NORM = 1.0 / float((RADIUS + 1) ** 6)
FIRST_FIX = 1.0 / (1.0 - 0.9**5)
SECOND_FIX = 1.0 / (1.0 - 0.999**5)
MESH = pl.DeviceIdType.MESH
ROUNDS = 3


def split(value):
    high = value.astype(jnp.bfloat16)
    low = (value - high.astype(jnp.float32)).astype(jnp.bfloat16)
    return high, low


def box(value):
    n = value.shape[0]
    two = value[: n - 1] + value[1:]
    four = two[: n - 3] + two[2:]
    eight = four[: n - 7] + four[4:]
    return eight[: n - 8] + value[8:]


def depth_matrix(length):
    row = lax.broadcasted_iota(jnp.int32, (2 * length, length), 0)
    col = lax.broadcasted_iota(jnp.int32, (2 * length, length), 1)
    row = jnp.where(row >= length, row - length, row)
    taps = jnp.maximum(RADIUS + 1 - jnp.abs(row - col), 0)
    return taps.astype(jnp.float32).astype(jnp.bfloat16)


def kernel(
    sizes,
    den,
    m1,
    m2,
    fwd,
    adj,
    weight,
    new_den,
    new_m1,
    new_m2,
    physical,
    ubuf,
    xbuf,
    sens,
    fbuf,
    abuf,
    m1buf,
    m2buf,
    local_sem,
    y_send,
    y_recv,
    t_send,
    t_recv,
    x_send,
    x_recv,
    s_send,
    s_recv,
):
    n_illum, n_gx, n_gy = sizes
    tile_x, tile_y, depth = den.shape
    sources, _, comps = fwd.shape[:3]
    groups = tile_x // RADIUS
    me = lax.axis_index("illum")
    gx = lax.axis_index("gx")
    gy = lax.axis_index("gy")
    odd = lax.rem(gx, 2)
    even = 1 - odd
    reach = tile_x - RADIUS
    starts = [even * (reach - 2 * RADIUS * j) + RADIUS * j for j in range(groups)]
    own = pl.ds(RADIUS, tile_y)

    loads = {}

    def load(name, src, dst):
        copy = pltpu.make_async_copy(src, dst, local_sem.at[len(loads)])
        copy.start()
        loads[name] = copy

    for j in range(groups):
        part = pl.ds(starts[j], RADIUS)
        load(("f", j), fwd.at[:, :, :, part], fbuf.at[:, :, :, part])
        load(("a", j), adj.at[:, :, :, part], abuf.at[:, :, :, part])
    load("d", den, ubuf.at[0, pl.ds(0, tile_x), own])
    load("m1", m1, m1buf)
    load("m2", m2, m2buf)

    pair = gx + even - odd
    beyond = gx - even + odd
    has_pair = jnp.logical_and(pair >= 0, pair < n_gx)
    has_beyond = jnp.logical_and(beyond >= 0, beyond < n_gx)
    pair = jnp.clip(pair, 0, n_gx - 1)
    beyond = jnp.clip(beyond, 0, n_gx - 1)
    y_there = (gy > 0, gy < n_gy - 1)
    y_at = (jnp.maximum(gy - 1, 0), jnp.minimum(gy + 1, n_gy - 1))
    y_device = [{"gy": at} for at in y_at]
    c_there = [jnp.logical_and(has_beyond, there) for there in y_there]
    c_device = [{"gx": beyond, "gy": at} for at in y_at]
    others = [{"illum": lax.rem(me + k, n_illum)} for k in range(1, n_illum)]

    barrier = pltpu.get_barrier_semaphore()
    greeted = [
        (y_there[0], y_device[0]),
        (y_there[1], y_device[1]),
        (has_pair, {"gx": pair}),
        (has_beyond, {"gx": beyond}),
        (c_there[0], c_device[0]),
        (c_there[1], c_device[1]),
    ]
    for there, device in greeted:

        @pl.when(there)
        def _(device=device):
            pl.semaphore_signal(barrier, inc=1, device_id=device, device_id_type=MESH)

    for device in others:
        pl.semaphore_signal(barrier, inc=1, device_id=device, device_id_type=MESH)

    for there, land in ((y_there[0], 0), (y_there[1], RADIUS + tile_y)):

        @pl.when(jnp.logical_not(there))
        def _(land=land):
            for r in range(ROUNDS):
                ubuf[r, :, pl.ds(land, RADIUS)] = jnp.zeros(
                    (tile_x + RADIUS, RADIUS, depth), jnp.float32
                )

    pair_land = even * (tile_x + RADIUS)
    beyond_land = odd * (tile_x + RADIUS)
    for there, land in ((has_pair, pair_land), (has_beyond, beyond_land)):

        @pl.when(jnp.logical_not(there))
        def _(land=land):
            for r in range(ROUNDS):
                xbuf[r, pl.ds(land, RADIUS)] = jnp.zeros(
                    (RADIUS, tile_y, depth), jnp.float32
                )

    z_taps = depth_matrix(depth)

    peers = jnp.int32(len(others))
    for there, _ in greeted:
        peers = peers + there.astype(jnp.int32)
    pl.semaphore_wait(barrier, peers)

    sent_rows = (RADIUS, tile_y)
    landing = (RADIUS + tile_y, 0)

    def rows_of(r, j, low, n, source):
        part = pl.ds(starts[j], RADIUS)
        if source is None:
            return ubuf.at[r, part, pl.ds(low, n)]
        return source.at[part, pl.ds(low - RADIUS, n)]

    def y_copy(r, d, j, source=None):
        return pltpu.make_async_remote_copy(
            src_ref=rows_of(r, j, sent_rows[d], RADIUS, source),
            dst_ref=ubuf.at[r, pl.ds(starts[j], RADIUS), pl.ds(landing[d], RADIUS)],
            send_sem=y_send.at[r, d, j],
            recv_sem=y_recv.at[r, d, j],
            device_id=y_device[d],
            device_id_type=MESH,
        )

    last = groups - 1

    def corner_copy(r, d, source=None):
        return pltpu.make_async_remote_copy(
            src_ref=rows_of(r, last, sent_rows[d], RADIUS, source),
            dst_ref=ubuf.at[r, pl.ds(tile_x, RADIUS), pl.ds(landing[d], RADIUS)],
            send_sem=t_send.at[r, d],
            recv_sem=t_recv.at[r, d],
            device_id=c_device[d],
            device_id_type=MESH,
        )

    def beyond_copy(r, source=None):
        return pltpu.make_async_remote_copy(
            src_ref=rows_of(r, last, RADIUS, tile_y, source),
            dst_ref=ubuf.at[r, pl.ds(tile_x, RADIUS), own],
            send_sem=t_send.at[r, 2],
            recv_sem=t_recv.at[r, 2],
            device_id={"gx": beyond},
            device_id_type=MESH,
        )

    def pair_copy(r, land):
        return pltpu.make_async_remote_copy(
            src_ref=xbuf.at[r, pl.ds(RADIUS + starts[0], RADIUS)],
            dst_ref=xbuf.at[r, pl.ds(land, RADIUS)],
            send_sem=x_send.at[r],
            recv_sem=x_recv.at[r],
            device_id={"gx": pair},
            device_id_type=MESH,
        )

    def s_copy(k, j, slot):
        part = pl.ds(starts[j], RADIUS)
        return pltpu.make_async_remote_copy(
            src_ref=sens.at[me, part],
            dst_ref=sens.at[slot, part],
            send_sem=s_send.at[k, j],
            recv_sem=s_recv.at[k, j],
            device_id=others[k],
            device_id_type=MESH,
        )

    def send(r, j, source=None):
        if j == last:
            for d in (0, 1):

                @pl.when(c_there[d])
                def _(d=d):
                    corner_copy(r, d, source).start()

            @pl.when(has_beyond)
            def _():
                beyond_copy(r, source).start()

        for d in (0, 1):

            @pl.when(y_there[d])
            def _(d=d):
                y_copy(r, d, j, source).start()

    for j in (last, *range(last)):
        send(0, j, den)

    for j in range(groups):
        loads["f", j].wait()
        loads["a", j].wait()
        for i in range(RADIUS):
            q = starts[j] + i
            total = None
            for s in range(sources):
                real = None
                for c in range(comps):
                    a = fbuf[s, 0, c, q].astype(jnp.float32) * abuf[s, 0, c, q].astype(
                        jnp.float32
                    )
                    b = fbuf[s, 1, c, q].astype(jnp.float32) * abuf[s, 1, c, q].astype(
                        jnp.float32
                    )
                    real = (a - b) if real is None else real + (a - b)
                term = weight[s] * real
                total = term if total is None else total + term
            sens[me, q] = total
        for k in range(len(others)):
            s_copy(k, j, me).start()

    def filter_rows(r, start, out):
        total = None
        for k in range(RADIUS + 1):
            row = ubuf[r, pl.ds(start, RADIUS), pl.ds(k, tile_y)]
            if k < RADIUS:
                row = row + ubuf[r, pl.ds(start, RADIUS), pl.ds(2 * RADIUS - k, tile_y)]
            row = row * float(k + 1)
            total = row if total is None else total + row
        xbuf[r, pl.ds(out, RADIUS)] = total

    def y_filter(r, j):
        for d, there in ((0, y_there[1]), (1, y_there[0])):

            @pl.when(there)
            def _(d=d):
                y_copy(r, d, j).wait_recv()

        filter_rows(r, starts[j], RADIUS + starts[j])
        if j == 0:

            @pl.when(has_pair)
            def _():
                pair_copy(r, odd * (tile_x + RADIUS)).start()

    def pair_arrive(r):
        @pl.when(has_pair)
        def _():
            pair_copy(r, pair_land).wait_recv()

    def beyond_filter(r):
        for d in (0, 1):

            @pl.when(c_there[1 - d])
            def _(d=d):
                corner_copy(r, d).wait_recv()

        @pl.when(has_beyond)
        def _():
            beyond_copy(r).wait_recv()
            filter_rows(r, tile_x, beyond_land)

    def xz_filter(r, j):
        value = xbuf[r, pl.ds(starts[j], 3 * RADIUS)]
        value = box(box(value)).reshape(RADIUS * tile_y, depth)
        both = jnp.concatenate(split(value), axis=1)
        out = jnp.dot(both, z_taps, preferred_element_type=jnp.float32)
        return (out * NORM).reshape(RADIUS, tile_y, depth)

    def chain(j, filtered):
        part = pl.ds(starts[j], RADIUS)
        for k in range(len(others)):
            s_copy(k, j, lax.rem(me + n_illum - 1 - k, n_illum)).wait_recv()
        total = sens[0, part]
        for e in range(1, n_illum):
            total = total + sens[e, part]
        inner = jnp.tanh(SHARPNESS * (filtered - THRESHOLD))
        ubuf[1, part, own] = total * (SHARPNESS * (1.0 - inner * inner) * (1.0 / SCALE))
        send(1, j)

    def update(j, gradient):
        part = pl.ds(starts[j], RADIUS)
        one = 0.9 * m1buf[part] + 0.1 * gradient
        two = 0.999 * m2buf[part] + 0.001 * gradient * gradient
        step = one * FIRST_FIX / (jnp.sqrt(two * SECOND_FIX) + 1e-08)
        value = jnp.clip(ubuf[0, part, own] - 0.05 * step, 0.0, 1.0)
        ubuf[2, part, own] = value
        send(2, j)
        new_m1[part] = one
        new_m2[part] = two
        new_den[part] = value

    def finish(j, value):
        part = pl.ds(starts[j], RADIUS)
        physical[part] = (TANH_EDGE + jnp.tanh(SHARPNESS * (value - THRESHOLD))) * (
            1.0 / SCALE
        )

    loads["d"].wait()
    for r, point in enumerate((chain, update, finish)):
        if r == 1:
            loads["m1"].wait()
            loads["m2"].wait()
        y_filter(r, 0)
        y_filter(r, 1)
        pair_arrive(r)
        point(0, xz_filter(r, 0))
        for j in range(2, groups):
            y_filter(r, j)
            point(j - 1, xz_filter(r, j - 1))
        beyond_filter(r)
        point(last, xz_filter(r, last))

    for j in range(groups):
        for k in range(len(others)):
            s_copy(k, j, me).wait_send()
    for r in range(ROUNDS):
        source = den if r == 0 else None
        for d in (0, 1):

            @pl.when(y_there[d])
            def _(d=d):
                for j in range(groups):
                    y_copy(r, d, j, source).wait_send()

            @pl.when(c_there[d])
            def _(d=d):
                corner_copy(r, d, source).wait_send()

        @pl.when(has_beyond)
        def _():
            beyond_copy(r, source).wait_send()

        @pl.when(has_pair)
        def _():
            pair_copy(r, odd * (tile_x + RADIUS)).wait_send()


def export(a, b, c, d, a_out, b_out, c_out, d_out, sem):
    copies = [
        pltpu.make_async_copy(src, dst, sem.at[i])
        for i, (src, dst) in enumerate(
            ((a, a_out), (b, b_out), (c, c_out), (d, d_out))
        )
    ]
    for copy in copies:
        copy.start()
    for copy in copies:
        copy.wait()


def shards(sizes, density, moment_one, moment_two, forward_field, adjoint_field, objective_weight):
    tile_x, tile_y, depth = density.shape
    n_illum = sizes[0]
    tile = jax.ShapeDtypeStruct(density.shape, jnp.float32)
    f32 = jnp.float32
    far = max(n_illum - 1, 1)
    groups = tile_x // RADIUS
    arguments = [
        pltpu.with_memory_space_constraint(x, pltpu.HBM)
        for x in (density, moment_one, moment_two, forward_field, adjoint_field)
    ]
    results = pl.pallas_call(
        functools.partial(kernel, sizes),
        out_shape=(pltpu.VMEM(density.shape, f32),) * 4,
        in_specs=[pl.BlockSpec(memory_space=pltpu.HBM)] * 5
        + [pl.BlockSpec(memory_space=pltpu.SMEM)],
        out_specs=(pl.BlockSpec(memory_space=pltpu.VMEM),) * 4,
        scratch_shapes=[
            pltpu.VMEM(
                (ROUNDS, tile_x + RADIUS, tile_y + 2 * RADIUS, depth), f32
            ),
            pltpu.VMEM((ROUNDS, tile_x + 2 * RADIUS, tile_y, depth), f32),
            pltpu.VMEM((n_illum, tile_x, tile_y, depth), f32),
            pltpu.VMEM(forward_field.shape, forward_field.dtype),
            pltpu.VMEM(adjoint_field.shape, adjoint_field.dtype),
            pltpu.VMEM(density.shape, f32),
            pltpu.VMEM(density.shape, f32),
            pltpu.SemaphoreType.DMA((2 * groups + 3,)),
            pltpu.SemaphoreType.DMA((ROUNDS, 2, groups)),
            pltpu.SemaphoreType.DMA((ROUNDS, 2, groups)),
            pltpu.SemaphoreType.DMA((ROUNDS, 3)),
            pltpu.SemaphoreType.DMA((ROUNDS, 3)),
            pltpu.SemaphoreType.DMA((ROUNDS,)),
            pltpu.SemaphoreType.DMA((ROUNDS,)),
            pltpu.SemaphoreType.DMA((far, groups)),
            pltpu.SemaphoreType.DMA((far, groups)),
        ],
        compiler_params=pltpu.CompilerParams(
            collective_id=0, has_side_effects=True, vmem_limit_bytes=48 << 20
        ),
        name="design_update",
    )(*arguments, objective_weight)
    return pl.pallas_call(
        export,
        out_shape=(tile,) * 4,
        in_specs=[pl.BlockSpec(memory_space=pltpu.VMEM)] * 4,
        out_specs=(pl.BlockSpec(memory_space=pl.ANY),) * 4,
        scratch_shapes=[pltpu.SemaphoreType.DMA((4,))],
        compiler_params=pltpu.CompilerParams(vmem_limit_bytes=4 << 20),
        name="export_results",
    )(*results)


def solution(mesh):
    field = P("illum", None, None, "gx", "gy", None)
    tile = P("gx", "gy", None)
    sizes = (mesh.shape["illum"], mesh.shape["gx"], mesh.shape["gy"])
    return jax.shard_map(
        functools.partial(shards, sizes),
        mesh=mesh,
        in_specs=(tile, tile, tile, field, field, P("illum")),
        out_specs=(tile,) * 4,
        check_vma=False,
    )
```

time: 26.2 us -> 23.5 us (0.90)
  the two profiles are of different devices: /device:TPU:1 before, /device:TPU:0 now
where the time goes in v1:
time: 23.5 us; the launch traced here: 23.3 us
  Pallas kernels  22 us (94%)
  between operations  1.29 us (5%)
    pallas_call x1, Pallas kernels, shards(): pl.pallas_call(functools.partial(kernel, sizes), out_shape=(pltpu.VMEM(de...  21 us
    pallas_call x1, Pallas kernels, shards(): pl.pallas_call(export, out_shape=(tile,) * 4, in_specs=[pl.BlockSpec(memo...  1 us

profile of v1, /device:TPU:0, one launch (start us, length us, event | category | flops | bytes accessed | tf_op | source)
XLA Modules:
  0.0 23.3 jit_solution(904183972864940389)
XLA Ops:
  1.3 21.0 %design_update.1 = (f32[32,16,128]{2,1,0:T(8,128)S(1)}, f32[32,16,128]{2,1,0:T(8,128)S(1)}, f32[32,16,128]{2,1,0:T(8,128)S(1)}, f32[32,16,128]{2,1,0:T(8,128)S(1)}) custom-call(f32[32,16,128]{2,1,0:T(8,128)} %den.1, f32[32,16,128]{2,1,0:T(8,128)} %m1.1, f32[32,16,128]{2,1,0:T(8,128)} %m2.1, bf16[1,2,3,32,16,128]{5,4,3,2,1,0:T(8,128)(2,1)} %fwd.1, ...), custom_call_target="tpu_custom_call" | custom-call | tf_op jit(solution)/shard_map/design_update/pallas_call | solution.py:406
  22.3 1.0 %export_results.1 = (f32[32,16,128]{2,1,0:T(8,128)}, f32[32,16,128]{2,1,0:T(8,128)}, f32[32,16,128]{2,1,0:T(8,128)}, f32[32,16,128]{2,1,0:T(8,128)}) custom-call(f32[32,16,128]{2,1,0:T(8,128)S(1)} %get-tuple-element.8.a, f32[32,16,128]{2,1,0:T(8,128)S(1)} %get-tuple-element.9.b, f32[32,16,128]{2,1,0:T(8,128)S(1)} %get-tuple-element.10.c, ...), custom_call_target="tpu_custom_call" | custom-call | tf_op jit(solution)/shard_map/export_results/pallas_call | solution.py:437

commit v2 on v1

--- a/solution.py
+++ b/solution.py
@@ -18,6 +18,14 @@
 SECOND_FIX = 1.0 / (1.0 - 0.999**5)
 MESH = pl.DeviceIdType.MESH
 ROUNDS = 3
+FIRST = (0, 1, 3, 2)
+SENS = (0, 1, 2, 3)
+LATE = (1, 2, 3)
+ORDERS = (
+    (("y", 0), ("late", 0), ("y", 1), ("pair", 0), ("out", 0), ("y", 2), ("out", 1), ("y", 3), ("out", 2), ("beyond", 0), ("out", 3), ),
+    (("y", 0), ("y", 1), ("pair", 0), ("out", 0), ("y", 2), ("out", 1), ("y", 3), ("out", 2), ("beyond", 0), ("out", 3), ),
+    (("y", 0), ("y", 1), ("pair", 0), ("out", 0), ("y", 2), ("out", 1), ("y", 3), ("out", 2), ("beyond", 0), ("out", 3), ),
+)
 
 
 def split(value):
@@ -220,6 +228,12 @@
         )
 
     def send(r, j, source=None):
+        for d in (0, 1):
+
+            @pl.when(y_there[d])
+            def _(d=d):
+                y_copy(r, d, j, source).start()
+
         if j == last:
             for d in (0, 1):
 
@@ -231,16 +245,10 @@
             def _():
                 beyond_copy(r, source).start()
 
-        for d in (0, 1):
-
-            @pl.when(y_there[d])
-            def _(d=d):
-                y_copy(r, d, j, source).start()
-
-    for j in (last, *range(last)):
+    for j in FIRST:
         send(0, j, den)
 
-    for j in range(groups):
+    for j in SENS:
         loads["f", j].wait()
         loads["a", j].wait()
         for i in range(RADIUS):
@@ -259,8 +267,16 @@
                 term = weight[s] * real
                 total = term if total is None else total + term
             sens[me, q] = total
-        for k in range(len(others)):
-            s_copy(k, j, me).start()
+        if j in LATE:
+
+            @pl.when(odd == 0)
+            def _(j=j):
+                for k in range(len(others)):
+                    s_copy(k, j, me).start()
+
+        else:
+            for k in range(len(others)):
+                s_copy(k, j, me).start()
 
     def filter_rows(r, start, out):
         total = None
@@ -344,15 +360,23 @@
         if r == 1:
             loads["m1"].wait()
             loads["m2"].wait()
-        y_filter(r, 0)
-        y_filter(r, 1)
-        pair_arrive(r)
-        point(0, xz_filter(r, 0))
-        for j in range(2, groups):
-            y_filter(r, j)
-            point(j - 1, xz_filter(r, j - 1))
-        beyond_filter(r)
-        point(last, xz_filter(r, last))
+        for step, j in ORDERS[r]:
+            if step == "y":
+                y_filter(r, j)
+            elif step == "pair":
+                pair_arrive(r)
+            elif step == "beyond":
+                beyond_filter(r)
+            elif step == "late":
+
+                @pl.when(odd == 1)
+                def _():
+                    for j in LATE:
+                        for k in range(len(others)):
+                            s_copy(k, j, me).start()
+
+            else:
+                point(j, xz_filter(r, j))
 
     for j in range(groups):
         for k in range(len(others)):

time: 23.5 us -> 23 us (0.979)
  the two profiles are of different devices: /device:TPU:0 before, /device:TPU:1 now
where the time goes in v2:
time: 23 us; the launch traced here: 22.9 us
  Pallas kernels  21.6 us (94%)
  between operations  1.29 us (6%)
    pallas_call x1, Pallas kernels, shards(): pl.pallas_call(functools.partial(kernel, sizes), out_shape=(pltpu.VMEM(de...  20.6 us
    pallas_call x1, Pallas kernels, shards(): pl.pallas_call(export, out_shape=(tile,) * 4, in_specs=[pl.BlockSpec(memo...  1 us

profile of v2, /device:TPU:1, one launch (start us, length us, event | category | flops | bytes accessed | tf_op | source)
XLA Modules:
  0.0 22.9 jit_solution(8005665053276396928)
XLA Ops:
  1.3 20.6 %design_update.1 = (f32[32,16,128]{2,1,0:T(8,128)S(1)}, f32[32,16,128]{2,1,0:T(8,128)S(1)}, f32[32,16,128]{2,1,0:T(8,128)S(1)}, f32[32,16,128]{2,1,0:T(8,128)S(1)}) custom-call(f32[32,16,128]{2,1,0:T(8,128)} %den.1, f32[32,16,128]{2,1,0:T(8,128)} %m1.1, f32[32,16,128]{2,1,0:T(8,128)} %m2.1, bf16[1,2,3,32,16,128]{5,4,3,2,1,0:T(8,128)(2,1)} %fwd.1, ...), custom_call_target="tpu_custom_call" | custom-call | tf_op jit(solution)/shard_map/design_update/pallas_call | solution.py:430
  21.9 1.0 %export_results.1 = (f32[32,16,128]{2,1,0:T(8,128)}, f32[32,16,128]{2,1,0:T(8,128)}, f32[32,16,128]{2,1,0:T(8,128)}, f32[32,16,128]{2,1,0:T(8,128)}) custom-call(f32[32,16,128]{2,1,0:T(8,128)S(1)} %get-tuple-element.8.a, f32[32,16,128]{2,1,0:T(8,128)S(1)} %get-tuple-element.9.b, f32[32,16,128]{2,1,0:T(8,128)S(1)} %get-tuple-element.10.c, ...), custom_call_target="tpu_custom_call" | custom-call | tf_op jit(solution)/shard_map/export_results/pallas_call | solution.py:461

commit v3 on v2

--- a/solution.py
+++ b/solution.py
@@ -23,8 +23,8 @@
 LATE = (1, 2, 3)
 ORDERS = (
     (("y", 0), ("late", 0), ("y", 1), ("pair", 0), ("out", 0), ("y", 2), ("out", 1), ("y", 3), ("out", 2), ("beyond", 0), ("out", 3), ),
-    (("y", 0), ("y", 1), ("pair", 0), ("out", 0), ("y", 2), ("out", 1), ("y", 3), ("out", 2), ("beyond", 0), ("out", 3), ),
-    (("y", 0), ("y", 1), ("pair", 0), ("out", 0), ("y", 2), ("out", 1), ("y", 3), ("out", 2), ("beyond", 0), ("out", 3), ),
+    (("y", 0), ("y", 1), ("pair", 0), ("out", 0), ("y", 2), ("out", 1), ("y", 3), ("beyond", 0), ("out", 3), ("out", 2), ),
+    (("y", 0), ("y", 1), ("y", 2), ("out", 1), ("y", 3), ("out", 2), ("pair", 0), ("out", 0), ("beyond", 0), ("out", 3), ),
 )
 
 
@@ -40,6 +40,18 @@
     four = two[: n - 3] + two[2:]
     eight = four[: n - 7] + four[4:]
     return eight[: n - 8] + value[8:]
+
+
+def project(value):
+    return (TANH_EDGE + jnp.tanh(SHARPNESS * (value - THRESHOLD))) * (1.0 / SCALE)
+
+
+def xz_rows(value, z_taps):
+    n, tile_y, depth = value.shape
+    value = box(box(value)).reshape((n - 2 * RADIUS) * tile_y, depth)
+    both = jnp.concatenate(split(value), axis=1)
+    out = jnp.dot(both, z_taps, preferred_element_type=jnp.float32)
+    return (out * NORM).reshape(n - 2 * RADIUS, tile_y, depth)
 
 
 def depth_matrix(length):
@@ -62,6 +74,7 @@
     new_m1,
     new_m2,
     physical,
+    tail,
     ubuf,
     xbuf,
     sens,
@@ -69,6 +82,7 @@
     abuf,
     m1buf,
     m2buf,
+    stage,
     local_sem,
     y_send,
     y_recv,
@@ -83,6 +97,7 @@
     tile_x, tile_y, depth = den.shape
     sources, _, comps = fwd.shape[:3]
     groups = tile_x // RADIUS
+    last = groups - 1
     me = lax.axis_index("illum")
     gx = lax.axis_index("gx")
     gy = lax.axis_index("gy")
@@ -91,21 +106,6 @@
     reach = tile_x - RADIUS
     starts = [even * (reach - 2 * RADIUS * j) + RADIUS * j for j in range(groups)]
     own = pl.ds(RADIUS, tile_y)
-
-    loads = {}
-
-    def load(name, src, dst):
-        copy = pltpu.make_async_copy(src, dst, local_sem.at[len(loads)])
-        copy.start()
-        loads[name] = copy
-
-    for j in range(groups):
-        part = pl.ds(starts[j], RADIUS)
-        load(("f", j), fwd.at[:, :, :, part], fbuf.at[:, :, :, part])
-        load(("a", j), adj.at[:, :, :, part], abuf.at[:, :, :, part])
-    load("d", den, ubuf.at[0, pl.ds(0, tile_x), own])
-    load("m1", m1, m1buf)
-    load("m2", m2, m2buf)
 
     pair = gx + even - odd
     beyond = gx - even + odd
@@ -129,14 +129,30 @@
         (c_there[0], c_device[0]),
         (c_there[1], c_device[1]),
     ]
+    for device in others:
+        pl.semaphore_signal(barrier, inc=1, device_id=device, device_id_type=MESH)
+
     for there, device in greeted:
 
         @pl.when(there)
         def _(device=device):
             pl.semaphore_signal(barrier, inc=1, device_id=device, device_id_type=MESH)
 
-    for device in others:
-        pl.semaphore_signal(barrier, inc=1, device_id=device, device_id_type=MESH)
+
+    loads = {}
+
+    def load(name, src, dst):
+        copy = pltpu.make_async_copy(src, dst, local_sem.at[len(loads)])
+        copy.start()
+        loads[name] = copy
+
+    for j in range(groups):
+        part = pl.ds(starts[j], RADIUS)
+        load(("f", j), fwd.at[:, :, :, part], fbuf.at[:, :, :, part])
+        load(("a", j), adj.at[:, :, :, part], abuf.at[:, :, :, part])
+    load("d", den, ubuf.at[0, pl.ds(0, tile_x), own])
+    load("m1", m1, m1buf)
+    load("m2", m2, m2buf)
 
     for there, land in ((y_there[0], 0), (y_there[1], RADIUS + tile_y)):
 
@@ -157,6 +173,14 @@
                 xbuf[r, pl.ds(land, RADIUS)] = jnp.zeros(
                     (RADIUS, tile_y, depth), jnp.float32
                 )
+
+    tail_at = {last: RADIUS, last - 1: 2 * RADIUS * even, groups: 2 * RADIUS * odd}
+
+    @pl.when(jnp.logical_not(has_beyond))
+    def _():
+        tail[pl.ds(tail_at[groups], RADIUS)] = jnp.zeros(
+            (RADIUS, tile_y, depth), jnp.float32
+        )
 
     z_taps = depth_matrix(depth)
 
@@ -183,8 +207,6 @@
             device_id=y_device[d],
             device_id_type=MESH,
         )
-
-    last = groups - 1
 
     def corner_copy(r, d, source=None):
         return pltpu.make_async_remote_copy(
@@ -228,6 +250,13 @@
         )
 
     def send(r, j, source=None):
+        if j == last:
+            for d in (0, 1):
+
+                @pl.when(c_there[d])
+                def _(d=d):
+                    corner_copy(r, d, source).start()
+
         for d in (0, 1):
 
             @pl.when(y_there[d])
@@ -235,11 +264,6 @@
                 y_copy(r, d, j, source).start()
 
         if j == last:
-            for d in (0, 1):
-
-                @pl.when(c_there[d])
-                def _(d=d):
-                    corner_copy(r, d, source).start()
 
             @pl.when(has_beyond)
             def _():
@@ -278,15 +302,23 @@
             for k in range(len(others)):
                 s_copy(k, j, me).start()
 
-    def filter_rows(r, start, out):
-        total = None
-        for k in range(RADIUS + 1):
-            row = ubuf[r, pl.ds(start, RADIUS), pl.ds(k, tile_y)]
-            if k < RADIUS:
-                row = row + ubuf[r, pl.ds(start, RADIUS), pl.ds(2 * RADIUS - k, tile_y)]
-            row = row * float(k + 1)
-            total = row if total is None else total + row
-        xbuf[r, pl.ds(out, RADIUS)] = total
+    def taps(ref, step, n):
+        one, two, three, four, five = (
+            ref[:, pl.ds(step * k, n)] for k in range(5)
+        )
+        return (one + five) + 2.0 * (two + four) + 3.0 * three
+
+    def store(r, out, j, total):
+        if r == ROUNDS - 1 and j in tail_at:
+            tail[pl.ds(tail_at[j], RADIUS)] = total
+        if r < ROUNDS - 1 or j <= last:
+            xbuf[r, pl.ds(out, RADIUS)] = total
+
+    def filter_rows(r, start, out, j):
+        near = pl.ds(0, tile_y + 12)
+        stage[:, near] = taps(ubuf.at[r, pl.ds(start, RADIUS)], 1, tile_y + 12)
+        total = taps(stage, 3, tile_y)
+        store(r, out, j, total)
 
     def y_filter(r, j):
         for d, there in ((0, y_there[1]), (1, y_there[0])):
@@ -295,7 +327,7 @@
             def _(d=d):
                 y_copy(r, d, j).wait_recv()
 
-        filter_rows(r, starts[j], RADIUS + starts[j])
+        filter_rows(r, starts[j], RADIUS + starts[j], j)
         if j == 0:
 
             @pl.when(has_pair)
@@ -317,14 +349,10 @@
         @pl.when(has_beyond)
         def _():
             beyond_copy(r).wait_recv()
-            filter_rows(r, tile_x, beyond_land)
+            filter_rows(r, tile_x, beyond_land, groups)
 
     def xz_filter(r, j):
-        value = xbuf[r, pl.ds(starts[j], 3 * RADIUS)]
-        value = box(box(value)).reshape(RADIUS * tile_y, depth)
-        both = jnp.concatenate(split(value), axis=1)
-        out = jnp.dot(both, z_taps, preferred_element_type=jnp.float32)
-        return (out * NORM).reshape(RADIUS, tile_y, depth)
+        return xz_rows(xbuf[r, pl.ds(starts[j], 3 * RADIUS)], z_taps)
 
     def chain(j, filtered):
         part = pl.ds(starts[j], RADIUS)
@@ -351,9 +379,7 @@
 
     def finish(j, value):
         part = pl.ds(starts[j], RADIUS)
-        physical[part] = (TANH_EDGE + jnp.tanh(SHARPNESS * (value - THRESHOLD))) * (
-            1.0 / SCALE
-        )
+        physical[part] = project(value)
 
     loads["d"].wait()
     for r, point in enumerate((chain, update, finish)):
@@ -375,7 +401,7 @@
                         for k in range(len(others)):
                             s_copy(k, j, me).start()
 
-            else:
+            elif r < ROUNDS - 1 or j < last:
                 point(j, xz_filter(r, j))
 
     for j in range(groups):
@@ -403,16 +429,24 @@
             pair_copy(r, odd * (tile_x + RADIUS)).wait_send()
 
 
-def export(a, b, c, d, a_out, b_out, c_out, d_out, sem):
+def export(a, b, c, d, tail, a_out, b_out, c_out, d_out, edge, sem):
+    tile_x = d.shape[0]
+    even = 1 - lax.rem(lax.axis_index("gx"), 2)
+    done = pl.ds(RADIUS * even, tile_x - RADIUS)
     copies = [
         pltpu.make_async_copy(src, dst, sem.at[i])
         for i, (src, dst) in enumerate(
-            ((a, a_out), (b, b_out), (c, c_out), (d, d_out))
+            ((d.at[done], d_out.at[done]), (a, a_out), (b, b_out), (c, c_out))
         )
     ]
     for copy in copies:
         copy.start()
-    for copy in copies:
+    edge[...] = project(xz_rows(tail[...], depth_matrix(d.shape[2])))
+    final = pltpu.make_async_copy(
+        edge, d_out.at[pl.ds((tile_x - RADIUS) * (1 - even), RADIUS)], sem.at[4]
+    )
+    final.start()
+    for copy in (*copies, final):
         copy.wait()
 
 
@@ -429,10 +463,11 @@
     ]
     results = pl.pallas_call(
         functools.partial(kernel, sizes),
-        out_shape=(pltpu.VMEM(density.shape, f32),) * 4,
+        out_shape=(pltpu.VMEM(density.shape, f32),) * 4
+        + (pltpu.VMEM((3 * RADIUS, tile_y, depth), f32),),
         in_specs=[pl.BlockSpec(memory_space=pltpu.HBM)] * 5
         + [pl.BlockSpec(memory_space=pltpu.SMEM)],
-        out_specs=(pl.BlockSpec(memory_space=pltpu.VMEM),) * 4,
+        out_specs=(pl.BlockSpec(memory_space=pltpu.VMEM),) * 5,
         scratch_shapes=[
             pltpu.VMEM(
                 (ROUNDS, tile_x + RADIUS, tile_y + 2 * RADIUS, depth), f32
@@ -443,6 +478,7 @@
             pltpu.VMEM(adjoint_field.shape, adjoint_field.dtype),
             pltpu.VMEM(density.shape, f32),
             pltpu.VMEM(density.shape, f32),
+            pltpu.VMEM((RADIUS, tile_y + 2 * RADIUS, depth), f32),
             pltpu.SemaphoreType.DMA((2 * groups + 3,)),
             pltpu.SemaphoreType.DMA((ROUNDS, 2, groups)),
             pltpu.SemaphoreType.DMA((ROUNDS, 2, groups)),
@@ -461,9 +497,12 @@
     return pl.pallas_call(
         export,
         out_shape=(tile,) * 4,
-        in_specs=[pl.BlockSpec(memory_space=pltpu.VMEM)] * 4,
+        in_specs=[pl.BlockSpec(memory_space=pltpu.VMEM)] * 5,
         out_specs=(pl.BlockSpec(memory_space=pl.ANY),) * 4,
-        scratch_shapes=[pltpu.SemaphoreType.DMA((4,))],
+        scratch_shapes=[
+            pltpu.VMEM((RADIUS, tile_y, depth), f32),
+            pltpu.SemaphoreType.DMA((5,)),
+        ],
         compiler_params=pltpu.CompilerParams(vmem_limit_bytes=4 << 20),
         name="export_results",
     )(*results)

time: 23 us -> 22.8 us (level)
    pallas_call x1, Pallas kernels: 20.6 us -> 20.3 us  [shards(): pl.pallas_call(functools.partial(kernel, sizes), out_shape=(pltpu.VMEM(de...]
where the time goes in v3:
time: 22.8 us; the launch traced here: 22.7 us
  Pallas kernels  21.4 us (94%)
  between operations  1.29 us (6%)
    pallas_call x1, Pallas kernels, shards(): pl.pallas_call(functools.partial(kernel, sizes), out_shape=(pltpu.VMEM(de...  20.3 us
    pallas_call x1, Pallas kernels, shards(): pl.pallas_call(export, out_shape=(tile,) * 4, in_specs=[pl.BlockSpec(memo...  1.08 us

profile of v3, /device:TPU:1, one launch (start us, length us, event | category | flops | bytes accessed | tf_op | source)
XLA Modules:
  0.0 22.7 jit_solution(16068686935751502981)
XLA Ops:
  1.3 20.3 %design_update.1 = (f32[32,16,128]{2,1,0:T(8,128)S(1)}, f32[32,16,128]{2,1,0:T(8,128)S(1)}, f32[32,16,128]{2,1,0:T(8,128)S(1)}, f32[32,16,128]{2,1,0:T(8,128)S(1)}, f32[24,16,128]{2,1,0:T(8,128)S(1)}) custom-call(f32[32,16,128]{2,1,0:T(8,128)} %den.1, f32[32,16,128]{2,1,0:T(8,128)} %m1.1, f32[32,16,128]{2,1,0:T(8,128)} %m2.1, ...), custom_call_target="tpu_custom_call" | custom-call | tf_op jit(solution)/shard_map/design_update/pallas_call | solution.py:464
  21.6 1.1 %export_results.1 = (f32[32,16,128]{2,1,0:T(8,128)}, f32[32,16,128]{2,1,0:T(8,128)}, f32[32,16,128]{2,1,0:T(8,128)}, f32[32,16,128]{2,1,0:T(8,128)}) custom-call(f32[32,16,128]{2,1,0:T(8,128)S(1)} %get-tuple-element.9.a, f32[32,16,128]{2,1,0:T(8,128)S(1)} %get-tuple-element.10.b, f32[32,16,128]{2,1,0:T(8,128)S(1)} %get-tuple-element.11.c, ...), custom_call_target="tpu_custom_call" | custom-call | tf_op jit(solution)/shard_map/export_results/pallas_call | solution.py:497

commit v4 on v3

--- a/solution.py
+++ b/solution.py
@@ -18,14 +18,20 @@
 SECOND_FIX = 1.0 / (1.0 - 0.999**5)
 MESH = pl.DeviceIdType.MESH
 ROUNDS = 3
-FIRST = (0, 1, 3, 2)
-SENS = (0, 1, 2, 3)
-LATE = (1, 2, 3)
-ORDERS = (
-    (("y", 0), ("late", 0), ("y", 1), ("pair", 0), ("out", 0), ("y", 2), ("out", 1), ("y", 3), ("out", 2), ("beyond", 0), ("out", 3), ),
-    (("y", 0), ("y", 1), ("pair", 0), ("out", 0), ("y", 2), ("out", 1), ("y", 3), ("beyond", 0), ("out", 3), ("out", 2), ),
-    (("y", 0), ("y", 1), ("y", 2), ("out", 1), ("y", 3), ("out", 2), ("pair", 0), ("out", 0), ("beyond", 0), ("out", 3), ),
-)
+LATE_FROM = 1
+
+
+def plan(groups):
+    last = groups - 1
+    sweep = [("y", 0), ("y", 1), ("pair", 0), ("out", 0)]
+    end = [("y", 0), ("y", 1)]
+    for j in range(2, groups):
+        sweep += [("y", j), ("out", j - 1)]
+        end += [("y", j), ("out", j - 1)]
+    first = sweep[:1] + [("late", 0)] + sweep[1:] + [("beyond", 0), ("out", last)]
+    second = sweep[:-1] + [("beyond", 0), ("out", last), ("out", last - 1)]
+    third = end + [("pair", 0), ("out", 0), ("beyond", 0), ("out", last)]
+    return first, second, third
 
 
 def split(value):
@@ -75,6 +81,7 @@
     new_m2,
     physical,
     tail,
+    z_taps,
     ubuf,
     xbuf,
     sens,
@@ -182,7 +189,7 @@
             (RADIUS, tile_y, depth), jnp.float32
         )
 
-    z_taps = depth_matrix(depth)
+    z_taps[...] = depth_matrix(depth)
 
     peers = jnp.int32(len(others))
     for there, _ in greeted:
@@ -269,10 +276,10 @@
             def _():
                 beyond_copy(r, source).start()
 
-    for j in FIRST:
+    for j in (0, 1, last, *range(2, last)):
         send(0, j, den)
 
-    for j in SENS:
+    for j in range(groups):
         loads["f", j].wait()
         loads["a", j].wait()
         for i in range(RADIUS):
@@ -291,7 +298,7 @@
                 term = weight[s] * real
                 total = term if total is None else total + term
             sens[me, q] = total
-        if j in LATE:
+        if j >= LATE_FROM:
 
             @pl.when(odd == 0)
             def _(j=j):
@@ -352,7 +359,7 @@
             filter_rows(r, tile_x, beyond_land, groups)
 
     def xz_filter(r, j):
-        return xz_rows(xbuf[r, pl.ds(starts[j], 3 * RADIUS)], z_taps)
+        return xz_rows(xbuf[r, pl.ds(starts[j], 3 * RADIUS)], z_taps[...])
 
     def chain(j, filtered):
         part = pl.ds(starts[j], RADIUS)
@@ -381,55 +388,64 @@
         part = pl.ds(starts[j], RADIUS)
         physical[part] = project(value)
 
+    def drain(r):
+        source = den if r == 0 else None
+        for d in (0, 1):
+
+            @pl.when(y_there[d])
+            def _(d=d):
+                for j in range(groups):
+                    y_copy(r, d, j, source).wait_send()
+
+            @pl.when(c_there[d])
+            def _(d=d):
+                corner_copy(r, d, source).wait_send()
+
+        @pl.when(has_beyond)
+        def _():
+            beyond_copy(r, source).wait_send()
+
+        @pl.when(has_pair)
+        def _():
+            pair_copy(r, odd * (tile_x + RADIUS)).wait_send()
+
+    def drain_early():
+        for j in range(groups):
+            for k in range(len(others)):
+                s_copy(k, j, me).wait_send()
+        for r in range(ROUNDS - 1):
+            drain(r)
+
     loads["d"].wait()
+    steps = plan(groups)
     for r, point in enumerate((chain, update, finish)):
         if r == 1:
             loads["m1"].wait()
             loads["m2"].wait()
-        for step, j in ORDERS[r]:
+        for step, j in steps[r]:
             if step == "y":
                 y_filter(r, j)
             elif step == "pair":
                 pair_arrive(r)
             elif step == "beyond":
+                if r == ROUNDS - 1:
+                    drain_early()
                 beyond_filter(r)
             elif step == "late":
 
                 @pl.when(odd == 1)
                 def _():
-                    for j in LATE:
+                    for j in range(LATE_FROM, groups):
                         for k in range(len(others)):
                             s_copy(k, j, me).start()
 
             elif r < ROUNDS - 1 or j < last:
                 point(j, xz_filter(r, j))
 
-    for j in range(groups):
-        for k in range(len(others)):
-            s_copy(k, j, me).wait_send()
-    for r in range(ROUNDS):
-        source = den if r == 0 else None
-        for d in (0, 1):
-
-            @pl.when(y_there[d])
-            def _(d=d):
-                for j in range(groups):
-                    y_copy(r, d, j, source).wait_send()
-
-            @pl.when(c_there[d])
-            def _(d=d):
-                corner_copy(r, d, source).wait_send()
-
-        @pl.when(has_beyond)
-        def _():
-            beyond_copy(r, source).wait_send()
-
-        @pl.when(has_pair)
-        def _():
-            pair_copy(r, odd * (tile_x + RADIUS)).wait_send()
-
-
-def export(a, b, c, d, tail, a_out, b_out, c_out, d_out, edge, sem):
+    drain(ROUNDS - 1)
+
+
+def export(a, b, c, d, tail, z_taps, a_out, b_out, c_out, d_out, edge, sem):
     tile_x = d.shape[0]
     even = 1 - lax.rem(lax.axis_index("gx"), 2)
     done = pl.ds(RADIUS * even, tile_x - RADIUS)
@@ -441,7 +457,7 @@
     ]
     for copy in copies:
         copy.start()
-    edge[...] = project(xz_rows(tail[...], depth_matrix(d.shape[2])))
+    edge[...] = project(xz_rows(tail[...], z_taps[...]))
     final = pltpu.make_async_copy(
         edge, d_out.at[pl.ds((tile_x - RADIUS) * (1 - even), RADIUS)], sem.at[4]
     )
@@ -464,10 +480,13 @@
     results = pl.pallas_call(
         functools.partial(kernel, sizes),
         out_shape=(pltpu.VMEM(density.shape, f32),) * 4
-        + (pltpu.VMEM((3 * RADIUS, tile_y, depth), f32),),
+        + (
+            pltpu.VMEM((3 * RADIUS, tile_y, depth), f32),
+            pltpu.VMEM((2 * depth, depth), jnp.bfloat16),
+        ),
         in_specs=[pl.BlockSpec(memory_space=pltpu.HBM)] * 5
         + [pl.BlockSpec(memory_space=pltpu.SMEM)],
-        out_specs=(pl.BlockSpec(memory_space=pltpu.VMEM),) * 5,
+        out_specs=(pl.BlockSpec(memory_space=pltpu.VMEM),) * 6,
         scratch_shapes=[
             pltpu.VMEM(
                 (ROUNDS, tile_x + RADIUS, tile_y + 2 * RADIUS, depth), f32
@@ -497,7 +516,7 @@
     return pl.pallas_call(
         export,
         out_shape=(tile,) * 4,
-        in_specs=[pl.BlockSpec(memory_space=pltpu.VMEM)] * 5,
+        in_specs=[pl.BlockSpec(memory_space=pltpu.VMEM)] * 6,
         out_specs=(pl.BlockSpec(memory_space=pl.ANY),) * 4,
         scratch_shapes=[
             pltpu.VMEM((RADIUS, tile_y, depth), f32),

time: 22.8 us -> 22.8 us (level)
  no operation moved by 1% of the time
where the time goes in v4:
time: 22.8 us; the launch traced here: 22.7 us
  Pallas kernels  21.4 us (94%)
  between operations  1.29 us (6%)
    pallas_call x1, Pallas kernels, shards(): pl.pallas_call(functools.partial(kernel, sizes), out_shape=(pltpu.VMEM(de...  20.3 us
    pallas_call x1, Pallas kernels, shards(): pl.pallas_call(export, out_shape=(tile,) * 4, in_specs=[pl.BlockSpec(memo...  1.06 us

profile of v4, /device:TPU:1, one launch (start us, length us, event | category | flops | bytes accessed | tf_op | source)
XLA Modules:
  0.0 22.7 jit_solution(12954159036849690056)
XLA Ops:
  1.3 20.3 %design_update.1 = (f32[32,16,128]{2,1,0:T(8,128)S(1)}, f32[32,16,128]{2,1,0:T(8,128)S(1)}, f32[32,16,128]{2,1,0:T(8,128)S(1)}, f32[32,16,128]{2,1,0:T(8,128)S(1...) custom-call(f32[32,16,128]{2,1,0:T(8,128)} %den.1, f32[32,16,128]{2,1,0:T(8,128)} %m1.1, f32[32,16,128]{2,1,0:T(8,128)} %m2.1, ...), custom_call_target="tpu_custom_call" | custom-call | tf_op jit(solution)/shard_map/design_update/pallas_call | solution.py:480
  21.6 1.1 %export_results.1 = (f32[32,16,128]{2,1,0:T(8,128)}, f32[32,16,128]{2,1,0:T(8,128)}, f32[32,16,128]{2,1,0:T(8,128)}, f32[32,16,128]{2,1,0:T(8,128)}) custom-call(f32[32,16,128]{2,1,0:T(8,128)S(1)} %get-tuple-element.10.a, f32[32,16,128]{2,1,0:T(8,128)S(1)} %get-tuple-element.11.b, f32[32,16,128]{2,1,0:T(8,128)S(1)} %get-tuple-element.12.c, ...), custom_call_target="tpu_custom_call" | custom-call | tf_op jit(solution)/shard_map/export_results/pallas_call | solution.py:516

commit v5 on v4

--- a/solution.py
+++ b/solution.py
@@ -28,7 +28,7 @@
     for j in range(2, groups):
         sweep += [("y", j), ("out", j - 1)]
         end += [("y", j), ("out", j - 1)]
-    first = sweep[:1] + [("late", 0)] + sweep[1:] + [("beyond", 0), ("out", last)]
+    first = sweep[:1] + [("late", 0)] + sweep[1:2] + [("late", 1)] + sweep[2:] + [("beyond", 0), ("out", last)]
     second = sweep[:-1] + [("beyond", 0), ("out", last), ("out", last - 1)]
     third = end + [("pair", 0), ("out", 0), ("beyond", 0), ("out", last)]
     return first, second, third
@@ -276,10 +276,13 @@
             def _():
                 beyond_copy(r, source).start()
 
-    for j in (0, 1, last, *range(2, last)):
+    for j in (0, 1):
         send(0, j, den)
 
     for j in range(groups):
+        if j == 1:
+            for i in (last, *range(2, last)):
+                send(0, i, den)
         loads["f", j].wait()
         loads["a", j].wait()
         for i in range(RADIUS):
@@ -434,8 +437,8 @@
             elif step == "late":
 
                 @pl.when(odd == 1)
-                def _():
-                    for j in range(LATE_FROM, groups):
+                def _(late=(range(1, 3), range(3, groups))[j]):
+                    for j in late:
                         for k in range(len(others)):
                             s_copy(k, j, me).start()
 

time: 22.8 us -> 22.8 us (level)
  no operation moved by 1% of the time
where the time goes in v5:
time: 22.8 us; the launch traced here: 22.7 us
  Pallas kernels  21.4 us (94%)
  between operations  1.29 us (6%)
    pallas_call x1, Pallas kernels, shards(): pl.pallas_call(functools.partial(kernel, sizes), out_shape=(pltpu.VMEM(de...  20.3 us
    pallas_call x1, Pallas kernels, shards(): pl.pallas_call(export, out_shape=(tile,) * 4, in_specs=[pl.BlockSpec(memo...  1.06 us

profile of v5, /device:TPU:1, one launch (start us, length us, event | category | flops | bytes accessed | tf_op | source)
XLA Modules:
  0.0 22.7 jit_solution(15920413890610210099)
XLA Ops:
  1.3 20.3 %design_update.1 = (f32[32,16,128]{2,1,0:T(8,128)S(1)}, f32[32,16,128]{2,1,0:T(8,128)S(1)}, f32[32,16,128]{2,1,0:T(8,128)S(1)}, f32[32,16,128]{2,1,0:T(8,128)S(1...) custom-call(f32[32,16,128]{2,1,0:T(8,128)} %den.1, f32[32,16,128]{2,1,0:T(8,128)} %m1.1, f32[32,16,128]{2,1,0:T(8,128)} %m2.1, ...), custom_call_target="tpu_custom_call" | custom-call | tf_op jit(solution)/shard_map/design_update/pallas_call | solution.py:483
  21.6 1.1 %export_results.1 = (f32[32,16,128]{2,1,0:T(8,128)}, f32[32,16,128]{2,1,0:T(8,128)}, f32[32,16,128]{2,1,0:T(8,128)}, f32[32,16,128]{2,1,0:T(8,128)}) custom-call(f32[32,16,128]{2,1,0:T(8,128)S(1)} %get-tuple-element.10.a, f32[32,16,128]{2,1,0:T(8,128)S(1)} %get-tuple-element.11.b, f32[32,16,128]{2,1,0:T(8,128)S(1)} %get-tuple-element.12.c, ...), custom_call_target="tpu_custom_call" | custom-call | tf_op jit(solution)/shard_map/export_results/pallas_call | solution.py:519

commit v6 on v5

--- a/solution.py
+++ b/solution.py
@@ -24,13 +24,12 @@
 def plan(groups):
     last = groups - 1
     sweep = [("y", 0), ("y", 1), ("pair", 0), ("out", 0)]
-    end = [("y", 0), ("y", 1)]
     for j in range(2, groups):
         sweep += [("y", j), ("out", j - 1)]
-        end += [("y", j), ("out", j - 1)]
     first = sweep[:1] + [("late", 0)] + sweep[1:2] + [("late", 1)] + sweep[2:] + [("beyond", 0), ("out", last)]
     second = sweep[:-1] + [("beyond", 0), ("out", last), ("out", last - 1)]
-    third = end + [("pair", 0), ("out", 0), ("beyond", 0), ("out", last)]
+    third = [("y", j) for j in range(groups)]
+    third += [("pair", 0), ("out", 0), ("middle", 0), ("beyond", 0)]
     return first, second, third
 
 
@@ -442,6 +441,11 @@
                         for k in range(len(others)):
                             s_copy(k, j, me).start()
 
+            elif step == "middle":
+                inner = xbuf[r, pl.ds(RADIUS, tile_x)]
+                physical[pl.ds(RADIUS, tile_x - 2 * RADIUS)] = project(
+                    xz_rows(inner, z_taps[...])
+                )
             elif r < ROUNDS - 1 or j < last:
                 point(j, xz_filter(r, j))
 

time: 22.8 us -> 22.5 us (0.987)
  Pallas kernels: 21.4 us -> 21 us
    pallas_call x1, Pallas kernels: 20.3 us -> 20 us  [shards(): pl.pallas_call(functools.partial(kernel, sizes), out_shape=(pltpu.VMEM(de...]
where the time goes in v6:
time: 22.5 us; the launch traced here: 22.3 us
  Pallas kernels  21 us (93%)
  between operations  1.29 us (6%)
    pallas_call x1, Pallas kernels, shards(): pl.pallas_call(functools.partial(kernel, sizes), out_shape=(pltpu.VMEM(de...  20 us
    pallas_call x1, Pallas kernels, shards(): pl.pallas_call(export, out_shape=(tile,) * 4, in_specs=[pl.BlockSpec(memo...  1.06 us

profile of v6, /device:TPU:1, one launch (start us, length us, event | category | flops | bytes accessed | tf_op | source)
XLA Modules:
  0.0 22.3 jit_solution(12468387486546303413)
XLA Ops:
  1.3 20.0 %design_update.1 = (f32[32,16,128]{2,1,0:T(8,128)S(1)}, f32[32,16,128]{2,1,0:T(8,128)S(1)}, f32[32,16,128]{2,1,0:T(8,128)S(1)}, f32[32,16,128]{2,1,0:T(8,128)S(1...) custom-call(f32[32,16,128]{2,1,0:T(8,128)} %den.1, f32[32,16,128]{2,1,0:T(8,128)} %m1.1, f32[32,16,128]{2,1,0:T(8,128)} %m2.1, ...), custom_call_target="tpu_custom_call" | custom-call | tf_op jit(solution)/shard_map/design_update/pallas_call | solution.py:487
  21.3 1.1 %export_results.1 = (f32[32,16,128]{2,1,0:T(8,128)}, f32[32,16,128]{2,1,0:T(8,128)}, f32[32,16,128]{2,1,0:T(8,128)}, f32[32,16,128]{2,1,0:T(8,128)}) custom-call(f32[32,16,128]{2,1,0:T(8,128)S(1)} %get-tuple-element.10.a, f32[32,16,128]{2,1,0:T(8,128)S(1)} %get-tuple-element.11.b, f32[32,16,128]{2,1,0:T(8,128)S(1)} %get-tuple-element.12.c, ...), custom_call_target="tpu_custom_call" | custom-call | tf_op jit(solution)/shard_map/export_results/pallas_call | solution.py:523

commit v7 on v6

--- a/solution.py
+++ b/solution.py
@@ -26,10 +26,11 @@
     sweep = [("y", 0), ("y", 1), ("pair", 0), ("out", 0)]
     for j in range(2, groups):
         sweep += [("y", j), ("out", j - 1)]
-    first = sweep[:1] + [("late", 0)] + sweep[1:2] + [("late", 1)] + sweep[2:] + [("beyond", 0), ("out", last)]
+    first = sweep[:1] + [("late", 0)] + sweep[1:2] + [("late", 1)] + sweep[2:-1]
+    first += [("beyond", 0), ("out", last - 1), ("out", last)]
     second = sweep[:-1] + [("beyond", 0), ("out", last), ("out", last - 1)]
     third = [("y", j) for j in range(groups)]
-    third += [("pair", 0), ("out", 0), ("middle", 0), ("beyond", 0)]
+    third += [("pair", 0), ("near", 0), ("beyond", 0)]
     return first, second, third
 
 
@@ -441,10 +442,11 @@
                         for k in range(len(others)):
                             s_copy(k, j, me).start()
 
-            elif step == "middle":
-                inner = xbuf[r, pl.ds(RADIUS, tile_x)]
-                physical[pl.ds(RADIUS, tile_x - 2 * RADIUS)] = project(
-                    xz_rows(inner, z_taps[...])
+            elif step == "near":
+                low = RADIUS * even
+                near = xbuf[r, pl.ds(low, tile_x + RADIUS)]
+                physical[pl.ds(low, tile_x - RADIUS)] = project(
+                    xz_rows(near, z_taps[...])
                 )
             elif r < ROUNDS - 1 or j < last:
                 point(j, xz_filter(r, j))

time: 22.5 us -> 22.5 us (level)
  no operation moved by 1% of the time
where the time goes in v7:
time: 22.5 us; the launch traced here: 22.3 us
  Pallas kernels  21 us (93%)
  between operations  1.29 us (6%)
    pallas_call x1, Pallas kernels, shards(): pl.pallas_call(functools.partial(kernel, sizes), out_shape=(pltpu.VMEM(de...  20 us
    pallas_call x1, Pallas kernels, shards(): pl.pallas_call(export, out_shape=(tile,) * 4, in_specs=[pl.BlockSpec(memo...  1.06 us

profile of v7, /device:TPU:1, one launch (start us, length us, event | category | flops | bytes accessed | tf_op | source)
XLA Modules:
  0.0 22.3 jit_solution(10701997421855802283)
XLA Ops:
  1.3 20.0 %design_update.1 = (f32[32,16,128]{2,1,0:T(8,128)S(1)}, f32[32,16,128]{2,1,0:T(8,128)S(1)}, f32[32,16,128]{2,1,0:T(8,128)S(1)}, f32[32,16,128]{2,1,0:T(8,128)S(1...) custom-call(f32[32,16,128]{2,1,0:T(8,128)} %den.1, f32[32,16,128]{2,1,0:T(8,128)} %m1.1, f32[32,16,128]{2,1,0:T(8,128)} %m2.1, ...), custom_call_target="tpu_custom_call" | custom-call | tf_op jit(solution)/shard_map/design_update/pallas_call | solution.py:489
  21.3 1.1 %export_results.1 = (f32[32,16,128]{2,1,0:T(8,128)}, f32[32,16,128]{2,1,0:T(8,128)}, f32[32,16,128]{2,1,0:T(8,128)}, f32[32,16,128]{2,1,0:T(8,128)}) custom-call(f32[32,16,128]{2,1,0:T(8,128)S(1)} %get-tuple-element.10.a, f32[32,16,128]{2,1,0:T(8,128)S(1)} %get-tuple-element.11.b, f32[32,16,128]{2,1,0:T(8,128)S(1)} %get-tuple-element.12.c, ...), custom_call_target="tpu_custom_call" | custom-call | tf_op jit(solution)/shard_map/export_results/pallas_call | solution.py:525

commit v8 on v6

--- a/solution.py
+++ b/solution.py
@@ -336,6 +336,10 @@
             def _(d=d):
                 y_copy(r, d, j).wait_recv()
 
+        if r == ROUNDS - 1 and 0 < j < last:
+            return
+        for i in range(1, last) if r == ROUNDS - 1 and j == last else ():
+            filter_rows(r, starts[i], RADIUS + starts[i], i)
         filter_rows(r, starts[j], RADIUS + starts[j], j)
         if j == 0:
 

time: 22.5 us -> 22.5 us (level)
  no operation moved by 1% of the time
where the time goes in v8:
time: 22.5 us; the launch traced here: 22.4 us
  Pallas kernels  21.1 us (94%)
  between operations  1.29 us (6%)
    pallas_call x1, Pallas kernels, shards(): pl.pallas_call(functools.partial(kernel, sizes), out_shape=(pltpu.VMEM(de...  20 us
    pallas_call x1, Pallas kernels, shards(): pl.pallas_call(export, out_shape=(tile,) * 4, in_specs=[pl.BlockSpec(memo...  1.06 us

profile of v8, /device:TPU:1, one launch (start us, length us, event | category | flops | bytes accessed | tf_op | source)
XLA Modules:
  0.0 22.4 jit_solution(4129730670163508645)
XLA Ops:
  1.3 20.0 %design_update.1 = (f32[32,16,128]{2,1,0:T(8,128)S(1)}, f32[32,16,128]{2,1,0:T(8,128)S(1)}, f32[32,16,128]{2,1,0:T(8,128)S(1)}, f32[32,16,128]{2,1,0:T(8,128)S(1...) custom-call(f32[32,16,128]{2,1,0:T(8,128)} %den.1, f32[32,16,128]{2,1,0:T(8,128)} %m1.1, f32[32,16,128]{2,1,0:T(8,128)} %m2.1, ...), custom_call_target="tpu_custom_call" | custom-call | tf_op jit(solution)/shard_map/design_update/pallas_call | solution.py:491
  21.3 1.1 %export_results.1 = (f32[32,16,128]{2,1,0:T(8,128)}, f32[32,16,128]{2,1,0:T(8,128)}, f32[32,16,128]{2,1,0:T(8,128)}, f32[32,16,128]{2,1,0:T(8,128)}) custom-call(f32[32,16,128]{2,1,0:T(8,128)S(1)} %get-tuple-element.10.a, f32[32,16,128]{2,1,0:T(8,128)S(1)} %get-tuple-element.11.b, f32[32,16,128]{2,1,0:T(8,128)S(1)} %get-tuple-element.12.c, ...), custom_call_target="tpu_custom_call" | custom-call | tf_op jit(solution)/shard_map/export_results/pallas_call | solution.py:527
